TPU v7x, 32 devices: a whole 2x2x4 slice. The times are simulated.
32 devices in a mesh: group: 8 (over y, x, core), tp: 4 (over z).
Axes of the slice: x: 2, y: 2, z: 4, core: 2. Of those that a mesh axis runs over, the one named last changes fastest.
Arguments:
- hidden: bfloat16 [2048, 8192], P('group', 'tp'), may hold values from -6 to 6
- w_kv: bfloat16 [8192, 2048], P('tp'), may hold values from -0.0625 to 0.0625
- prompt_lengths: int32 [2, 8], replicated, may hold values from 1 to 128, 256 in all within a row
- owner_step: int32 [2, 8], replicated, may hold values from 1 to 3
- cache: bfloat16 [64, 128, 2048], P(('group', 'tp')), may hold values from -8 to 8
- cache_len: int32 [64], P(('group', 'tp')), may hold values from 1 to 128
- queries: bfloat16 [64, 8192], P('group', 'tp'), may hold values from -200 to 200
- fresh: bfloat16 [64, 2048], P('group', 'tp'), may hold values from -10 to 10
- logits: bfloat16 [64, 30720], P('group', 'tp'), may hold values from -300 to 300
- states: int32 [64], P('group'), may hold values from 0 to 23
- masks: int32 [24, 1024], P(None, 'tp'), may hold values from 0 to 1073741823, as said below
Outputs:
- attended: bfloat16 [64, 8192], P('group', 'tp')
- logprob: float32 [64, 30720], P('group', 'tp')
Inputs may be any that keep to these rules, and one draw needn't show every extreme that they name: `prompt_lengths`: each row sums to 256; the longest prompt of every row has exactly 128 tokens. Prompt k of prefill group p goes to group p + owner_step[p, k] * 2. `masks`: every state allows at least one token in each aligned block of 7680 vocabulary entries.
All inputs are finite; a program needn't handle non-finite values.
Results may differ from a plain program's by a relative error of at most 0.02.
Values may be sent and summed in bfloat16 or wider, within the bound.
A program may use at most 64 MiB of HBM per device.

v0:
```python
import math
import jax
import jax.numpy as jnp
from jax import lax
from jax.sharding import PartitionSpec as P

HEADS = 64
KVH = 8
HD = 128
MAXLEN = 128
CACHE = 128
STATES = 24


def from_behind(block, axis, distance):
    devices = range(lax.axis_size(axis))
    route = [(i - distance, i) for i in devices if i - distance in devices]
    return lax.ppermute(block, axis, route)


def landing(slot_ids, source, turn_index, prompt_lengths, owner_step):
    chosen = owner_step[source] == turn_index
    ranking = jnp.cumsum(chosen.astype(jnp.int32)) - 1
    arrivals = jnp.sum(chosen.astype(jnp.int32))
    matched = chosen[None, :] & (ranking[None, :] == slot_ids[:, None])
    lengths = prompt_lengths[source]
    starts = jnp.cumsum(lengths) - lengths
    first_row = jnp.sum(jnp.where(matched, starts[None, :], 0), axis=1)
    prompt_len = jnp.sum(jnp.where(matched, lengths[None, :], 0), axis=1)
    landed = (slot_ids < arrivals) & (turn_index >= 1)
    return (landed, first_row, prompt_len)


def attend(query_rows, merged, alive_len, fresh_rows):
    row_count = merged.shape[0]
    group_size = HEADS // KVH
    key_rows = merged[:, :, : KVH * HD].reshape(row_count, CACHE, KVH, HD)
    value_rows = merged[:, :, KVH * HD :].reshape(row_count, CACHE, KVH, HD)
    queries = query_rows.reshape(row_count, KVH, group_size, HD)
    own_key = fresh_rows[:, : KVH * HD].reshape(row_count, KVH, HD)
    own_value = fresh_rows[:, KVH * HD :].reshape(row_count, KVH, HD)
    scaling = 1.0 / math.sqrt(HD)
    scores = (
        jnp.einsum("rkgd,rtkd->rkgt", queries, key_rows, preferred_element_type=jnp.float32)
        * scaling
    )
    own_score = (
        jnp.einsum("rkgd,rkd->rkg", queries, own_key, preferred_element_type=jnp.float32) * scaling
    )
    positions = jnp.arange(CACHE, dtype=jnp.int32)
    alive_mask = (positions[None, :] < alive_len[:, None])[:, None, None, :]
    highest = jnp.maximum(jnp.max(jnp.where(alive_mask, scores, -jnp.inf), axis=3), own_score)
    exponent = jnp.where(alive_mask, jnp.exp(scores - highest[..., None]), 0.0)
    own_exponent = jnp.exp(own_score - highest)
    denominator = jnp.sum(exponent, axis=3) + own_exponent
    weights = (exponent / denominator[..., None]).astype(jnp.bfloat16)
    own_weight = (own_exponent / denominator).astype(jnp.bfloat16)
    attended = jnp.einsum(
        "rkgt,rtkd->rkgd", weights, value_rows, preferred_element_type=jnp.float32
    )
    attended = (
        attended
        + own_weight.astype(jnp.float32)[..., None] * own_value.astype(jnp.float32)[:, :, None, :]
    )
    return attended.reshape(row_count, HEADS * HD).astype(jnp.bfloat16)


def per_device(
    hidden,
    w_kv,
    prompt_lengths,
    owner_step,
    cache,
    cache_len,
    queries,
    fresh,
    logits,
    states,
    masks,
):
    tensor_size = lax.axis_size("tp")
    groups = lax.axis_size("group")
    prefill = groups // 4
    group_index = lax.axis_index("group")
    column = lax.axis_index("tp")
    is_prefill = group_index < prefill
    source = group_index % prefill
    turn_index = group_index // prefill
    token_count = hidden.shape[0]
    kv_width = w_kv.shape[1]
    own_count = cache.shape[0]
    own_slots = jnp.arange(own_count, dtype=jnp.int32) * tensor_size + column
    landed, first_row, prompt_len = landing(
        own_slots, source, turn_index, prompt_lengths, owner_step
    )

    def compute():
        return jnp.dot(hidden, w_kv, preferred_element_type=jnp.float32)

    kv_piece = lax.psum_scatter(
        lax.cond(
            is_prefill,
            compute,
            lambda: jnp.zeros(
                (token_count // tensor_size * lax.axis_size("tp"), kv_width), jnp.float32
            ),
        ).astype(jnp.bfloat16),
        "tp",
        scatter_dimension=0,
        tiled=True,
    )
    arrived = [from_behind(kv_piece, "group", prefill * step_index) for step_index in (1, 2, 3)]
    incoming = jnp.where(
        turn_index == 1, arrived[0], jnp.where(turn_index == 2, arrived[1], arrived[2])
    )
    gathered = lax.all_gather(incoming, "tp", axis=0, tiled=True)
    padded = jnp.pad(gathered, ((0, MAXLEN), (0, 0)))
    handed = jax.vmap(lambda offset: lax.dynamic_slice_in_dim(padded, offset, MAXLEN, 0))(first_row)
    front = jnp.where(landed[:, None, None], handed, cache)
    merged = jnp.concatenate([front, cache[:, MAXLEN:]], axis=1)
    alive_len = jnp.where(landed, prompt_len, cache_len)
    mine_queries, mine_fresh = (
        lax.all_to_all(queries, "tp", split_axis=0, concat_axis=1, tiled=True),
        lax.all_to_all(fresh, "tp", split_axis=0, concat_axis=1, tiled=True),
    )
    attended = attend(mine_queries, merged, alive_len, mine_fresh)
    attended = lax.all_to_all(attended, "tp", split_axis=1, concat_axis=0, tiled=True)
    onehot = states[:, None] == jnp.arange(STATES, dtype=jnp.int32)[None, :]
    packed = jnp.sum(jnp.where(onehot[:, :, None], masks[None, :, :], 0), axis=1)
    shifts = jnp.arange(30, dtype=jnp.int32)
    bit_flags = jnp.bitwise_and(jnp.right_shift(packed[:, :, None], shifts[None, None, :]), 1)
    permitted = bit_flags.reshape(packed.shape[0], logits.shape[1]) == 1
    values = logits.astype(jnp.float32)
    local_peak = jnp.max(jnp.where(permitted, values, -jnp.inf), axis=1)
    highest = lax.pmax(local_peak, "tp")
    local_terms = jnp.sum(jnp.where(permitted, jnp.exp(values - highest[:, None]), 0.0), axis=1)
    denominator = lax.psum(local_terms, "tp")
    normalizer = highest + jnp.log(denominator)
    logprob = jnp.where(permitted, values - normalizer[:, None], 0.0)
    return (attended, logprob)


def solution(mesh):
    in_specs = (
        P("group", "tp"),
        P("tp", None),
        P(),
        P(),
        P(("group", "tp"), None, None),
        P(("group", "tp")),
        P("group", "tp"),
        P("group", "tp"),
        P("group", "tp"),
        P("group"),
        P(None, "tp"),
    )
    out_specs = (P("group", "tp"), P("group", "tp"))
    return jax.shard_map(
        per_device, mesh=mesh, in_specs=in_specs, out_specs=out_specs, check_vma=False
    )
```

profile of v0, /device:TPU:0, one launch (start us, length us, event | category | flops | bytes accessed | tf_op | source)
XLA Modules:
  0.0 112.0 jit_solution(17203343120737466503)
XLA Ops:
  7.3 6.1 %conditional.1 = (bf16[256,2048]{1,0:T(8,128)(2,1)S(1)}) conditional(s32[]{:T(128)} %convert_element_type.47, () %tuple.14, (bf16[256,2048]{1,0:T(8,128)(2,1)}, bf16[2048,2048]{1,0:T(8,128)(2,1)}) %tuple.15), branch_computations={%region_3.4_spmd, %region_4.5_spmd} | conditional | flops 2147483648 | bytes 10485768 | solution.py:101
  7.3 6.1 %fusion.24 = bf16[256,2048]{1,0:T(8,128)(2,1)S(1)} fusion(bf16[256,2048]{1,0:T(8,128)(2,1)} %get-tuple-element.13, bf16[2048,2048]{1,0:T(8,128)(2,1)} %get-tuple-element.14), kind=kOutput, calls=%fused_computation.57 | convolution fusion | flops 2147483648 | bytes 10485760 | tf_op jit(solution)/shard_map/cond/branch_1_fun/dot_general | solution.py:98
  13.5 1.0 copy-done
  14.5 0.6 all_to_all.41
  15.1 6.3 %all-to-all-start.1 = ((bf16[4,2,512]{2,1,0:T(2,128)(2,1)}), bf16[4,2,512]{2,1,0:T(2,128)(2,1)S(1)}, u32[]{:S(2)}, u32[]{:S(2)}) async-start(bf16[4,2,512]{2,1,0:T(2,128)(2,1)} %all_to_all.41), calls=%async_computation.2 | async-start | bytes 16384 | tf_op jit(solution)/shard_map/all_to_all | solution.py:124
  21.5 0.1 select_reduce_fusion
  21.6 0.3 shift_right_arithmetic.20
  22.0 0.5 shift_right_arithmetic.21
  22.5 0.1 shift_right_arithmetic.23
  22.6 0.2 fusion.1
  22.8 12.6 %pmax.7 = f32[8]{0:T(128)S(1)} all-reduce(f32[8]{0:T(128)S(1)} %get-tuple-element.49), channel_id=1, replica_groups=mesh['group'=8,'tp'=4] {'tp'}, use_global_device_ids=true, to_apply=%region_12.13 | all-reduce | flops 8 | bytes 64 | tf_op jit(solution)/shard_map/pmax | solution.py:135
  35.5 0.2 reduce-window_1_clone.1
  35.7 0.3 fusion.4
  35.9 7.2 %reduce-scatter.2.cloned.1.call-done = bf16[64,2048]{1,0:T(8,128)(2,1)} async-done(((bf16[256,2048]{1,0:T(8,128)(2,1)}), bf16[64,2048]{1,0:T(8,128)(2,1)}) %reduce-scatter.2.cloned.1.call-update) | async-done | bytes 262160 | tf_op jit(solution)/shard_map/reduce_scatter | solution.py:100
  43.1 3.1 %collective-permute-start = (bf16[64,2048]{1,0:T(8,128)(2,1)}, bf16[64,2048]{1,0:T(8,128)(2,1)S(1)}, u32[]{:S(2)}, u32[]{:S(2)}) collective-permute-start(bf16[64,2048]{1,0:T(8,128)(2,1)} %reduce-scatter.2.cloned.1.call-done), channel_id=1, source_target_pairs={{0,8},{4,12},{8,16},{12,20},{16,24},{20,28},{1,9},{5,13},{9,17},{1... | collective-permute-start | bytes 786440 | tf_op jit(solution)/shard_map/ppermute | solution.py:18
  46.2 3.4 %collective-permute-start.1 = (bf16[64,2048]{1,0:T(8,128)(2,1)}, bf16[64,2048]{1,0:T(8,128)(2,1)S(1)}, u32[]{:S(2)}, u32[]{:S(2)}) collective-permute-start(bf16[64,2048]{1,0:T(8,128)(2,1)} %reduce-scatter.2.cloned.1.call-done), channel_id=1, source_target_pairs={{0,16},{4,20},{8,24},{12,28},{1,17},{5,21},{9,25},{13,29},{2,18},{... | collective-permute-start | bytes 786440 | tf_op jit(solution)/shard_map/ppermute | solution.py:18
  49.6 1.3 %collective-permute-start.2 = (bf16[64,2048]{1,0:T(8,128)(2,1)}, bf16[64,2048]{1,0:T(8,128)(2,1)S(1)}, u32[]{:S(2)}, u32[]{:S(2)}) collective-permute-start(bf16[64,2048]{1,0:T(8,128)(2,1)} %reduce-scatter.2.cloned.1.call-done), channel_id=1, source_target_pairs={{0,24},{4,28},{1,25},{5,29},{2,26},{6,30},{3,27},{7,31}} | collective-permute-start | bytes 786440 | tf_op jit(solution)/shard_map/ppermute | solution.py:18
  51.0 0.2 reduce-window.9
  51.2 1.7 %collective-permute-done = bf16[64,2048]{1,0:T(8,128)(2,1)S(1)} collective-permute-done((bf16[64,2048]{1,0:T(8,128)(2,1)}, bf16[64,2048]{1,0:T(8,128)(2,1)S(1)}, u32[]{:S(2)}, u32[]{:S(2)}) %collective-permute-start) | collective-permute-done | bytes 262176 | tf_op jit(solution)/shard_map/ppermute | solution.py:18
  52.9 5.3 %collective-permute-done.1 = bf16[64,2048]{1,0:T(8,128)(2,1)S(1)} collective-permute-done((bf16[64,2048]{1,0:T(8,128)(2,1)}, bf16[64,2048]{1,0:T(8,128)(2,1)S(1)}, u32[]{:S(2)}, u32[]{:S(2)}) %collective-permute-start.1) | collective-permute-done | bytes 262176 | tf_op jit(solution)/shard_map/ppermute | solution.py:18
  58.2 0.8 select_select_fusion
  59.0 9.2 %psum.7 = f32[8]{0:T(128)S(1)} all-reduce(f32[8]{0:T(128)S(1)} %fusion.4), channel_id=1, replica_groups=mesh['group'=8,'tp'=4] {'tp'}, use_global_device_ids=true, to_apply=%region_14.15 | all-reduce | flops 8 | bytes 64 | tf_op jit(solution)/shard_map/psum | solution.py:137
  68.2 0.6 fusion.19
  68.8 0.2 fusion.16
  69.0 0.7 fusion.21
  69.9 1.3 %copy.34 = bf16[2,128,2048]{1,2,0:T(8,128)(2,1)} copy(bf16[2,128,2048]{2,1,0:T(8,128)(2,1)S(1)} %copy-done.2) | data formatting | bytes 2097152 | tf_op args[4]
  71.2 0.6 all_to_all.38
  71.8 3.3 %all-to-all-start = ((bf16[4,2,2048]{2,1,0:T(2,128)(2,1)}), bf16[4,2,2048]{2,1,0:T(2,128)(2,1)S(1)}, u32[]{:S(2)}, u32[]{:S(2)}) async-start(bf16[4,2,2048]{2,1,0:T(2,128)(2,1)} %all_to_all.38), calls=%async_computation.1 | async-start | bytes 65536 | tf_op jit(solution)/shard_map/all_to_all | solution.py:123
  75.2 6.0 %all-to-all-done = bf16[4,2,2048]{2,1,0:T(2,128)(2,1)S(1)} async-done(((bf16[4,2,2048]{2,1,0:T(2,128)(2,1)}), bf16[4,2,2048]{2,1,0:T(2,128)(2,1)S(1)}, u32[]{:S(2)}, u32[]{:S(2)}) %all-to-all-start) | async-done | bytes 32800 | tf_op jit(solution)/shard_map/all_to_all | solution.py:123
  81.2 0.1 fusion.25
  81.3 6.8 %all-gather.2.cloned.1.call-done = bf16[256,2048]{1,0:T(8,128)(2,1)} async-done(((bf16[64,2048]{1,0:T(8,128)(2,1)}), bf16[256,2048]{1,0:T(8,128)(2,1)}) %all-gather.2.cloned.1.call-update) | async-done | bytes 1048592 | tf_op jit(solution)/shard_map/all_gather | solution.py:116
  88.2 1.4 %pad.5 = bf16[384,2048]{1,0:T(8,128)(2,1)S(1)} pad(bf16[256,2048]{1,0:T(8,128)(2,1)} %all-gather.2.cloned.1.call-done, bf16[]{:T(256)} %constant.55.clone.1), padding=0_128x0_0 | pad | bytes 2621442 | tf_op jit(solution)/shard_map/jit(_pad)/pad | solution.py:117
  89.6 2.7 %while.1 = (s32[]{:T(128)}, bf16[384,2048]{1,0:T(8,128)(2,1)S(1)}, s32[2,2]{1,0:T(2,128)S(1)}, bf16[2,128,2048]{1,2,0:T(8,128)(2,1)}, s32[]{:T(128)}) while((s32[]{:T(128)}, bf16[384,2048]{1,0:T(8,128)(2,1)S(1)}, s32[2,2]{1,0:T(2,128)S(1)}, bf16[2,128,2048]{1,2,0:T(8,128)(2,1)}, s32[]{:T(128)}) %tuple.40), condition=%wide.while_cond, body=%wide.while_body.sunk | while | flops 2 | bytes 3146325 | solution.py:118
  89.6 0.2 dynamic-slice_bitcast_fusion.2
  89.8 0.3 copy.51
  90.0 0.9 constant_dynamic-update-slice_fusion.2
  90.9 0.2 dynamic-slice_bitcast_fusion.2
  91.1 0.3 copy.51
  91.4 0.9 constant_dynamic-update-slice_fusion.2
  92.2 1.7 %broadcast_select_fusion = bf16[2,128,2048]{1,2,0:T(8,128)(2,1)S(1)} fusion(bf16[2,128,2048]{1,2,0:T(8,128)(2,1)} %get-tuple-element.22, bf16[2,128,2048]{1,2,0:T(8,128)(2,1)} %copy.34, pred[2]{0:T(512)(128)(4,1)S(1)} %get-tuple-element.52), kind=kLoop, calls=%fused_computation.6 | loop fusion | flops 524288 | bytes 3145730 | tf_op jit(solution)/shard_map/jit(_where)/select_n | solution.py:119
  94.0 0.3 select_reduce_fusion.1
  94.3 0.2 bitcast_reduce_fusion
  94.5 0.4 fusion
  95.0 0.7 copy.38
  95.6 3.3 %all-to-all-start.2 = ((bf16[2,4,2048]{2,0,1:T(2,128)(2,1)}), bf16[2,4,2048]{2,0,1:T(2,128)(2,1)S(1)}, u32[]{:S(2)}, u32[]{:S(2)}) async-start(bf16[2,4,2048]{2,0,1:T(2,128)(2,1)} %copy.38), calls=%async_computation.3 | async-start | bytes 65536 | tf_op jit(solution)/shard_map/all_to_all | solution.py:127
  98.9 0.8 fusion.5
  99.7 4.8 %all-to-all-done.2 = bf16[2,4,2048]{2,0,1:T(2,128)(2,1)S(1)} async-done(((bf16[2,4,2048]{2,0,1:T(2,128)(2,1)}), bf16[2,4,2048]{2,0,1:T(2,128)(2,1)S(1)}, u32[]{:S(2)}, u32[]{:S(2)}) %all-to-all-start.2) | async-done | bytes 32800 | tf_op jit(solution)/shard_map/all_to_all | solution.py:127
  104.5 0.6 all_to_all.47
  (50 shorter events, 0.6 us)
Async XLA Ops:
  7.2 35.9 %reduce-scatter.2.cloned.1.call-start = ((), (), s32[]{:S(2)}) async-start(), calls=%async_computation.4 | async-start | bytes 1310720 | tf_op jit(solution)/shard_map/reduce_scatter | solution.py:100
  7.2 7.3 %copy-start.5 = (bf16[8,512]{1,0:T(8,128)(2,1)S(1)}, bf16[8,512]{1,0:T(8,128)(2,1)}, u32[]{:S(2)}) copy-start(bf16[8,512]{1,0:T(8,128)(2,1)} %param.20) | copy-start | bytes 24580
  7.2 14.2 %copy-start.9 = (s32[8]{0:T(128)S(1)}, s32[8]{0:T(128)}, u32[]{:S(2)}) copy-start(s32[8]{0:T(128)} %param.22) | copy-start | bytes 100
  7.2 14.3 %copy-start.4 = (s32[24,256]{1,0:T(8,128)S(1)}, s32[24,256]{1,0:T(8,128)}, u32[]{:S(2)}) copy-start(s32[24,256]{1,0:T(8,128)} %param.23) | copy-start | bytes 73732
  7.3 15.4 %copy-start.1 = (bf16[8,7680]{1,0:T(8,128)(2,1)S(1)}, bf16[8,7680]{1,0:T(8,128)(2,1)}, u32[]{:S(2)}) copy-start(bf16[8,7680]{1,0:T(8,128)(2,1)} %param.21) | copy-start | bytes 368644
  7.3 28.2 %copy-start.8 = (s32[2,8]{1,0:T(2,128)S(1)}, s32[2,8]{1,0:T(2,128)}, u32[]{:S(2)}) copy-start(s32[2,8]{1,0:T(2,128)} %param.15) | copy-start | bytes 196
  7.3 43.7 %copy-start.6 = (s32[2,8]{1,0:T(2,128)S(1)}, s32[2,8]{1,0:T(2,128)}, u32[]{:S(2)}) copy-start(s32[2,8]{1,0:T(2,128)} %param.16) | copy-start | bytes 196
  7.3 61.7 %copy-start.7 = (s32[2]{0:T(128)S(1)}, s32[2]{0:T(128)}, u32[]{:S(2)}) copy-start(s32[2]{0:T(128)} %param.18) | copy-start | bytes 28
  7.3 62.6 %copy-start.2 = (bf16[2,128,2048]{2,1,0:T(8,128)(2,1)S(1)}, bf16[2,128,2048]{2,1,0:T(8,128)(2,1)}, u32[]{:S(2)}) copy-start(bf16[2,128,2048]{2,1,0:T(8,128)(2,1)} %param.17) | copy-start | bytes 3145732
  7.3 63.9 %copy-start.3 = (bf16[8,2048]{1,0:T(8,128)(2,1)S(1)}, bf16[8,2048]{1,0:T(8,128)(2,1)}, u32[]{:S(2)}) copy-start(bf16[8,2048]{1,0:T(8,128)(2,1)} %param.19) | copy-start | bytes 98308
  13.5 1.0 copy-start
  15.1 56.7 %all-to-all-start.1 = ((bf16[4,2,512]{2,1,0:T(2,128)(2,1)}), bf16[4,2,512]{2,1,0:T(2,128)(2,1)S(1)}, u32[]{:S(2)}, u32[]{:S(2)}) async-start(bf16[4,2,512]{2,1,0:T(2,128)(2,1)} %all_to_all.41), calls=%async_computation.2 | async-start | bytes 16384 | tf_op jit(solution)/shard_map/all_to_all | solution.py:124
  21.5 66.7 %all-gather.2.cloned.1.call-start = ((), (), s32[]{:S(2)}) async-start(), calls=%async_computation.5 | async-start | bytes 1310720 | tf_op jit(solution)/shard_map/all_gather | solution.py:116
  43.1 9.8 %collective-permute-start = (bf16[64,2048]{1,0:T(8,128)(2,1)}, bf16[64,2048]{1,0:T(8,128)(2,1)S(1)}, u32[]{:S(2)}, u32[]{:S(2)}) collective-permute-start(bf16[64,2048]{1,0:T(8,128)(2,1)} %reduce-scatter.2.cloned.1.call-done), channel_id=1, source_target_pairs={{0,8},{4,12},{8,16},{12,20},{16,24},{20,28},{1,9},{5,13},{9,17},{1... | collective-permute-start | bytes 786440 | tf_op jit(solution)/shard_map/ppermute | solution.py:18
  46.2 12.0 %collective-permute-start.1 = (bf16[64,2048]{1,0:T(8,128)(2,1)}, bf16[64,2048]{1,0:T(8,128)(2,1)S(1)}, u32[]{:S(2)}, u32[]{:S(2)}) collective-permute-start(bf16[64,2048]{1,0:T(8,128)(2,1)} %reduce-scatter.2.cloned.1.call-done), channel_id=1, source_target_pairs={{0,16},{4,20},{8,24},{12,28},{1,17},{5,21},{9,25},{13,29},{2,18},{... | collective-permute-start | bytes 786440 | tf_op jit(solution)/shard_map/ppermute | solution.py:18
  49.6 8.6 %collective-permute-start.2 = (bf16[64,2048]{1,0:T(8,128)(2,1)}, bf16[64,2048]{1,0:T(8,128)(2,1)S(1)}, u32[]{:S(2)}, u32[]{:S(2)}) collective-permute-start(bf16[64,2048]{1,0:T(8,128)(2,1)} %reduce-scatter.2.cloned.1.call-done), channel_id=1, source_target_pairs={{0,24},{4,28},{1,25},{5,29},{2,26},{6,30},{3,27},{7,31}} | collective-permute-start | bytes 786440 | tf_op jit(solution)/shard_map/ppermute | solution.py:18
  71.8 9.3 %all-to-all-start = ((bf16[4,2,2048]{2,1,0:T(2,128)(2,1)}), bf16[4,2,2048]{2,1,0:T(2,128)(2,1)S(1)}, u32[]{:S(2)}, u32[]{:S(2)}) async-start(bf16[4,2,2048]{2,1,0:T(2,128)(2,1)} %all_to_all.38), calls=%async_computation.1 | async-start | bytes 65536 | tf_op jit(solution)/shard_map/all_to_all | solution.py:123
  95.6 8.9 %all-to-all-start.2 = ((bf16[2,4,2048]{2,0,1:T(2,128)(2,1)}), bf16[2,4,2048]{2,0,1:T(2,128)(2,1)S(1)}, u32[]{:S(2)}, u32[]{:S(2)}) async-start(bf16[2,4,2048]{2,0,1:T(2,128)(2,1)} %copy.38), calls=%async_computation.3 | async-start | bytes 65536 | tf_op jit(solution)/shard_map/all_to_all | solution.py:127
Sparse Core Ops, SparseCore 0:
  14.6 28.4 reduce-scatter.1
  59.1 28.9 all-gather.1
where the time goes:
time: 113 us; the launch traced here: 112 us
  waiting for transfers between devices  31.9 us (28%)
  blocking collectives  21.8 us (19%)
  starting transfers between devices  20.7 us (18%)
  between operations  14.3 us (13%)
  local copies, waits for them, and re-layouts  10.1 us (9%)
  matrix products  7 us (6%)
  other arithmetic  6.08 us (5%)
    pmax x1, blocking collectives, per_device(): highest = lax.pmax(local_peak, 'tp')  12.6 us
    psum x1, blocking collectives, per_device(): denominator = lax.psum(local_terms, 'tp')  9.17 us
    ppermute x3, starting transfers between devices, from_behind(): return lax.ppermute(block, axis, route)  7.82 us
    reduce_scatter x1, waiting for transfers between devices, per_device(): lax.psum_scatter(lax.cond(is_prefill, compute, lambda: jnp.zeros((token_c...  7.16 us
    ppermute x3, waiting for transfers between devices, from_behind(): return lax.ppermute(block, axis, route)  7.05 us
    all_gather x1, waiting for transfers between devices, per_device(): gathered = lax.all_gather(incoming, 'tp', axis=0, tiled=True)  6.82 us
    all_to_all x1, starting transfers between devices, per_device(): lax.all_to_all(fresh, 'tp', split_axis=0, concat_axis=1, tiled=True)  6.35 us
    dot_general x1, matrix products, compute(): return jnp.dot(hidden, w_kv, preferred_element_type=jnp.float32)  6.13 us
  transfers between devices with their start and end apart: 8, of which 6 were waited for; matrix products, arithmetic and copies ran while one was open for 6% of the time, Pallas kernels for 0%

commit v1 on v0

--- a/solution.py
+++ b/solution.py
@@ -3,6 +3,7 @@
 import jax.numpy as jnp
 from jax import lax
 from jax.sharding import PartitionSpec as P
+from jax.lax import axis_size, ppermute
 
 HEADS = 64
 KVH = 8
@@ -78,6 +79,23 @@
     states,
     masks,
 ):
+
+    def obtain_the_gates(comm_axis, work_x):
+        amount_of = axis_size(comm_axis)
+
+        def enter_patches(prior, s_next):
+            if s_next >= amount_of:
+                return prior
+            local_part = enter_patches(
+                prior
+                + ppermute(prior, comm_axis, tuple(((ix, ix ^ s_next) for ix in range(amount_of)))),
+                2 * s_next,
+            )
+            return local_part
+
+        f_now = enter_patches(work_x, 1)
+        return f_now
+
     tensor_size = lax.axis_size("tp")
     groups = lax.axis_size("group")
     prefill = groups // 4
@@ -134,7 +152,7 @@
     local_peak = jnp.max(jnp.where(permitted, values, -jnp.inf), axis=1)
     highest = lax.pmax(local_peak, "tp")
     local_terms = jnp.sum(jnp.where(permitted, jnp.exp(values - highest[:, None]), 0.0), axis=1)
-    denominator = lax.psum(local_terms, "tp")
+    denominator = obtain_the_gates("tp", local_terms)
     normalizer = highest + jnp.log(denominator)
     logprob = jnp.where(permitted, values - normalizer[:, None], 0.0)
     return (attended, logprob)

time: 113 us -> 112 us (level)
  blocking collectives: 21.8 us -> 12.6 us
  waiting for transfers between devices: 31.9 us -> 39.7 us
  starting transfers between devices: 20.7 us -> 22.2 us
    psum x1 -> x0, blocking collectives: 9.17 us -> none  [per_device(): denominator = lax.psum(local_terms, 'tp')]
    all_gather x1, waiting for transfers between devices: 6.82 us -> 11.6 us  [per_device(): gathered = lax.all_gather(incoming, 'tp', axis=0, tiled=True)]
    ppermute x0 -> x2, waiting for transfers between devices: none -> 3.2 us  [enter_patches(): ppermute(prior, comm_axis, tuple(((ix, ix ^ s_next) for ix in range(amoun...]
    ppermute x0 -> x2, starting transfers between devices: none -> 1.39 us  [enter_patches(): ppermute(prior, comm_axis, tuple(((ix, ix ^ s_next) for ix in range(amoun...]
  transfers between devices with their start and end apart: 8 -> 10, of which waited for: 6 -> 7; matrix products, arithmetic and copies ran while one was open for 6% -> 6% of each run, Pallas kernels for 0% -> 0%
where the time goes in v1:
time: 112 us
  waiting for transfers between devices  39.7 us (35%)
  starting transfers between devices  22.2 us (20%)
  between operations  14.4 us (13%)
  blocking collectives  12.6 us (11%)
  local copies, waits for them, and re-layouts  10 us (9%)
  matrix products  7 us (6%)
  other arithmetic  5.98 us (5%)
    pmax x1, blocking collectives, per_device(): highest = lax.pmax(local_peak, 'tp')  12.6 us
    all_gather x1, waiting for transfers between devices, per_device(): gathered = lax.all_gather(incoming, 'tp', axis=0, tiled=True)  11.6 us
    ppermute x3, starting transfers between devices, from_behind(): return lax.ppermute(block, axis, route)  7.83 us
    reduce_scatter x1, waiting for transfers between devices, per_device(): lax.psum_scatter(lax.cond(is_prefill, compute, lambda: jnp.zeros((token_c...  7.04 us
    ppermute x3, waiting for transfers between devices, from_behind(): return lax.ppermute(block, axis, route)  7.01 us
    all_to_all x1, starting transfers between devices, per_device(): lax.all_to_all(fresh, 'tp', split_axis=0, concat_axis=1, tiled=True)  6.35 us
    dot_general x1, matrix products, compute(): return jnp.dot(hidden, w_kv, preferred_element_type=jnp.float32)  6.13 us
    all_to_all x1, waiting for transfers between devices, per_device(): lax.all_to_all(queries, 'tp', split_axis=0, concat_axis=1, tiled=True)  5.96 us
  transfers between devices with their start and end apart: 10, of which 7 were waited for; matrix products, arithmetic and copies ran while one was open for 6% of the time, Pallas kernels for 0%

profile of v1, /device:TPU:0, one launch (start us, length us, event | category | flops | bytes accessed | tf_op | source)
XLA Modules:
  0.0 112.0 jit_solution(4605166776224155049)
XLA Ops:
  7.3 6.1 %conditional.1 = (bf16[256,2048]{1,0:T(8,128)(2,1)S(1)}) conditional(s32[]{:T(128)} %convert_element_type.47, () %tuple.14, (bf16[256,2048]{1,0:T(8,128)(2,1)}, bf16[2048,2048]{1,0:T(8,128)(2,1)}) %tuple.15), branch_computations={%region_3.4_spmd, %region_4.5_spmd} | conditional | flops 2147483648 | bytes 10485768 | solution.py:119
  7.3 6.1 %fusion.24 = bf16[256,2048]{1,0:T(8,128)(2,1)S(1)} fusion(bf16[256,2048]{1,0:T(8,128)(2,1)} %get-tuple-element.13, bf16[2048,2048]{1,0:T(8,128)(2,1)} %get-tuple-element.14), kind=kOutput, calls=%fused_computation.57 | convolution fusion | flops 2147483648 | bytes 10485760 | tf_op jit(solution)/shard_map/cond/branch_1_fun/dot_general | solution.py:116
  13.5 1.0 copy-done
  14.5 0.6 all_to_all.41
  15.1 6.3 %all-to-all-start.1 = ((bf16[4,2,512]{2,1,0:T(2,128)(2,1)}), bf16[4,2,512]{2,1,0:T(2,128)(2,1)S(1)}, u32[]{:S(2)}, u32[]{:S(2)}) async-start(bf16[4,2,512]{2,1,0:T(2,128)(2,1)} %all_to_all.41), calls=%async_computation.2 | async-start | bytes 16384 | tf_op jit(solution)/shard_map/all_to_all | solution.py:142
  21.6 0.3 shift_right_arithmetic.20
  22.0 0.5 shift_right_arithmetic.21
  22.5 0.1 shift_right_arithmetic.23
  22.6 0.2 fusion.1
  22.8 12.6 %pmax.7 = f32[8]{0:T(128)S(1)} all-reduce(f32[8]{0:T(128)S(1)} %get-tuple-element.49), channel_id=1, replica_groups=mesh['group'=8,'tp'=4] {'tp'}, use_global_device_ids=true, to_apply=%region_12.13 | all-reduce | flops 8 | bytes 64 | tf_op jit(solution)/shard_map/pmax | solution.py:153
  35.4 0.3 fusion.4
  35.8 0.2 reduce-window_1_clone.1
  36.0 7.0 %reduce-scatter.2.cloned.1.call-done = bf16[64,2048]{1,0:T(8,128)(2,1)} async-done(((bf16[256,2048]{1,0:T(8,128)(2,1)}), bf16[64,2048]{1,0:T(8,128)(2,1)}) %reduce-scatter.2.cloned.1.call-update) | async-done | bytes 262160 | tf_op jit(solution)/shard_map/reduce_scatter | solution.py:118
  43.1 3.1 %collective-permute-start = (bf16[64,2048]{1,0:T(8,128)(2,1)}, bf16[64,2048]{1,0:T(8,128)(2,1)S(1)}, u32[]{:S(2)}, u32[]{:S(2)}) collective-permute-start(bf16[64,2048]{1,0:T(8,128)(2,1)} %reduce-scatter.2.cloned.1.call-done), channel_id=1, source_target_pairs={{0,8},{4,12},{8,16},{12,20},{16,24},{20,28},{1,9},{5,13},{9,17},{1... | collective-permute-start | bytes 786440 | tf_op jit(solution)/shard_map/ppermute | solution.py:19
  46.2 3.4 %collective-permute-start.1 = (bf16[64,2048]{1,0:T(8,128)(2,1)}, bf16[64,2048]{1,0:T(8,128)(2,1)S(1)}, u32[]{:S(2)}, u32[]{:S(2)}) collective-permute-start(bf16[64,2048]{1,0:T(8,128)(2,1)} %reduce-scatter.2.cloned.1.call-done), channel_id=1, source_target_pairs={{0,16},{4,20},{8,24},{12,28},{1,17},{5,21},{9,25},{13,29},{2,18},{... | collective-permute-start | bytes 786440 | tf_op jit(solution)/shard_map/ppermute | solution.py:19
  49.6 1.3 %collective-permute-start.2 = (bf16[64,2048]{1,0:T(8,128)(2,1)}, bf16[64,2048]{1,0:T(8,128)(2,1)S(1)}, u32[]{:S(2)}, u32[]{:S(2)}) collective-permute-start(bf16[64,2048]{1,0:T(8,128)(2,1)} %reduce-scatter.2.cloned.1.call-done), channel_id=1, source_target_pairs={{0,24},{4,28},{1,25},{5,29},{2,26},{6,30},{3,27},{7,31}} | collective-permute-start | bytes 786440 | tf_op jit(solution)/shard_map/ppermute | solution.py:19
  51.0 0.2 reduce-window.9
  51.2 1.7 %collective-permute-done = bf16[64,2048]{1,0:T(8,128)(2,1)S(1)} collective-permute-done((bf16[64,2048]{1,0:T(8,128)(2,1)}, bf16[64,2048]{1,0:T(8,128)(2,1)S(1)}, u32[]{:S(2)}, u32[]{:S(2)}) %collective-permute-start) | collective-permute-done | bytes 262176 | tf_op jit(solution)/shard_map/ppermute | solution.py:19
  52.9 5.3 %collective-permute-done.1 = bf16[64,2048]{1,0:T(8,128)(2,1)S(1)} collective-permute-done((bf16[64,2048]{1,0:T(8,128)(2,1)}, bf16[64,2048]{1,0:T(8,128)(2,1)S(1)}, u32[]{:S(2)}, u32[]{:S(2)}) %collective-permute-start.1) | collective-permute-done | bytes 262176 | tf_op jit(solution)/shard_map/ppermute | solution.py:19
  58.2 0.7 select_select_fusion
  59.0 0.2 fusion.16
  59.3 1.3 %copy.34 = bf16[2,128,2048]{1,2,0:T(8,128)(2,1)} copy(bf16[2,128,2048]{2,1,0:T(8,128)(2,1)S(1)} %copy-done.2) | data formatting | bytes 2097152 | tf_op args[4]
  60.6 0.6 all_to_all.38
  61.2 0.6 fusion.19
  61.9 0.6 fusion.21
  62.5 1.3 %collective-permute-start.4 = (f32[8]{0:T(128)S(1)}, f32[8]{0:T(128)S(1)}, u32[]{:S(2)}, u32[]{:S(2)}) collective-permute-start(f32[8]{0:T(128)S(1)} %add.67), channel_id=1, source_target_pairs={{0,2},{1,3},{2,0},{3,1},{4,6},{5,7},{6,4},{7,5},{8,10},{9,11},{10,... | collective-permute-start | bytes 104 | tf_op jit(solution)/shard_map/ppermute | solution.py:91
  63.9 3.2 %collective-permute-done.4 = f32[8]{0:T(128)S(1)} collective-permute-done((f32[8]{0:T(128)S(1)}, f32[8]{0:T(128)S(1)}, u32[]{:S(2)}, u32[]{:S(2)}) %collective-permute-start.4) | collective-permute-done | bytes 64 | tf_op jit(solution)/shard_map/ppermute | solution.py:91
  67.1 3.3 %all-to-all-start = ((bf16[4,2,2048]{2,1,0:T(2,128)(2,1)}), bf16[4,2,2048]{2,1,0:T(2,128)(2,1)S(1)}, u32[]{:S(2)}, u32[]{:S(2)}) async-start(bf16[4,2,2048]{2,1,0:T(2,128)(2,1)} %all_to_all.38), calls=%async_computation.1 | async-start | bytes 65536 | tf_op jit(solution)/shard_map/all_to_all | solution.py:141
  70.4 6.0 %all-to-all-done = bf16[4,2,2048]{2,1,0:T(2,128)(2,1)S(1)} async-done(((bf16[4,2,2048]{2,1,0:T(2,128)(2,1)}), bf16[4,2,2048]{2,1,0:T(2,128)(2,1)S(1)}, u32[]{:S(2)}, u32[]{:S(2)}) %all-to-all-start) | async-done | bytes 32800 | tf_op jit(solution)/shard_map/all_to_all | solution.py:141
  76.4 0.1 fusion.25
  76.5 11.6 %all-gather.2.cloned.1.call-done = bf16[256,2048]{1,0:T(8,128)(2,1)} async-done(((bf16[64,2048]{1,0:T(8,128)(2,1)}), bf16[256,2048]{1,0:T(8,128)(2,1)}) %all-gather.2.cloned.1.call-update) | async-done | bytes 1048592 | tf_op jit(solution)/shard_map/all_gather | solution.py:134
  88.1 1.4 %pad.5 = bf16[384,2048]{1,0:T(8,128)(2,1)S(1)} pad(bf16[256,2048]{1,0:T(8,128)(2,1)} %all-gather.2.cloned.1.call-done, bf16[]{:T(256)} %constant.55.clone.1), padding=0_128x0_0 | pad | bytes 2621442 | tf_op jit(solution)/shard_map/jit(_pad)/pad | solution.py:135
  89.5 2.6 %while.1 = (s32[]{:T(128)}, bf16[384,2048]{1,0:T(8,128)(2,1)S(1)}, s32[2,2]{1,0:T(2,128)S(1)}, bf16[2,128,2048]{1,2,0:T(8,128)(2,1)}, s32[]{:T(128)}) while((s32[]{:T(128)}, bf16[384,2048]{1,0:T(8,128)(2,1)S(1)}, s32[2,2]{1,0:T(2,128)S(1)}, bf16[2,128,2048]{1,2,0:T(8,128)(2,1)}, s32[]{:T(128)}) %tuple.40), condition=%wide.while_cond, body=%wide.while_body.sunk | while | flops 2 | bytes 3146325 | solution.py:136
  89.6 0.2 dynamic-slice_bitcast_fusion.2
  89.7 0.3 copy.51
  90.0 0.8 constant_dynamic-update-slice_fusion.2
  90.9 0.2 dynamic-slice_bitcast_fusion.2
  91.0 0.3 copy.51
  91.3 0.8 constant_dynamic-update-slice_fusion.2
  92.2 1.7 %broadcast_select_fusion = bf16[2,128,2048]{1,2,0:T(8,128)(2,1)S(1)} fusion(bf16[2,128,2048]{1,2,0:T(8,128)(2,1)} %get-tuple-element.22, bf16[2,128,2048]{1,2,0:T(8,128)(2,1)} %copy.34, pred[2]{0:T(512)(128)(4,1)S(1)} %get-tuple-element.52), kind=kLoop, calls=%fused_computation.6 | loop fusion | flops 524288 | bytes 3145730 | tf_op jit(solution)/shard_map/jit(_where)/select_n | solution.py:137
  94.0 0.3 select_reduce_fusion.1
  94.3 0.2 bitcast_reduce_fusion
  94.5 0.4 fusion
  95.0 0.7 copy.38
  95.6 3.3 %all-to-all-start.2 = ((bf16[2,4,2048]{2,0,1:T(2,128)(2,1)}), bf16[2,4,2048]{2,0,1:T(2,128)(2,1)S(1)}, u32[]{:S(2)}, u32[]{:S(2)}) async-start(bf16[2,4,2048]{2,0,1:T(2,128)(2,1)} %copy.38), calls=%async_computation.3 | async-start | bytes 65536 | tf_op jit(solution)/shard_map/all_to_all | solution.py:145
  98.9 0.8 fusion.5
  99.7 4.8 %all-to-all-done.2 = bf16[2,4,2048]{2,0,1:T(2,128)(2,1)S(1)} async-done(((bf16[2,4,2048]{2,0,1:T(2,128)(2,1)}), bf16[2,4,2048]{2,0,1:T(2,128)(2,1)S(1)}, u32[]{:S(2)}, u32[]{:S(2)}) %all-to-all-start.2) | async-done | bytes 32800 | tf_op jit(solution)/shard_map/all_to_all | solution.py:145
  104.5 0.6 all_to_all.47
  (54 shorter events, 0.8 us)
Async XLA Ops:
  7.2 35.9 %reduce-scatter.2.cloned.1.call-start = ((), (), s32[]{:S(2)}) async-start(), calls=%async_computation.4 | async-start | bytes 1310720 | tf_op jit(solution)/shard_map/reduce_scatter | solution.py:118
  7.2 7.2 %copy-start.5 = (bf16[8,512]{1,0:T(8,128)(2,1)S(1)}, bf16[8,512]{1,0:T(8,128)(2,1)}, u32[]{:S(2)}) copy-start(bf16[8,512]{1,0:T(8,128)(2,1)} %param.20) | copy-start | bytes 24580
  7.2 14.2 %copy-start.9 = (s32[8]{0:T(128)S(1)}, s32[8]{0:T(128)}, u32[]{:S(2)}) copy-start(s32[8]{0:T(128)} %param.22) | copy-start | bytes 100
  7.2 14.3 %copy-start.4 = (s32[24,256]{1,0:T(8,128)S(1)}, s32[24,256]{1,0:T(8,128)}, u32[]{:S(2)}) copy-start(s32[24,256]{1,0:T(8,128)} %param.23) | copy-start | bytes 73732
  7.3 15.4 %copy-start.1 = (bf16[8,7680]{1,0:T(8,128)(2,1)S(1)}, bf16[8,7680]{1,0:T(8,128)(2,1)}, u32[]{:S(2)}) copy-start(bf16[8,7680]{1,0:T(8,128)(2,1)} %param.21) | copy-start | bytes 368644
  7.3 28.6 %copy-start.8 = (s32[2,8]{1,0:T(2,128)S(1)}, s32[2,8]{1,0:T(2,128)}, u32[]{:S(2)}) copy-start(s32[2,8]{1,0:T(2,128)} %param.15) | copy-start | bytes 196
  7.3 43.7 %copy-start.6 = (s32[2,8]{1,0:T(2,128)S(1)}, s32[2,8]{1,0:T(2,128)}, u32[]{:S(2)}) copy-start(s32[2,8]{1,0:T(2,128)} %param.16) | copy-start | bytes 196
  7.3 52.0 %copy-start.2 = (bf16[2,128,2048]{2,1,0:T(8,128)(2,1)S(1)}, bf16[2,128,2048]{2,1,0:T(8,128)(2,1)}, u32[]{:S(2)}) copy-start(bf16[2,128,2048]{2,1,0:T(8,128)(2,1)} %param.17) | copy-start | bytes 3145732
  7.3 53.3 %copy-start.3 = (bf16[8,2048]{1,0:T(8,128)(2,1)S(1)}, bf16[8,2048]{1,0:T(8,128)(2,1)}, u32[]{:S(2)}) copy-start(bf16[8,2048]{1,0:T(8,128)(2,1)} %param.19) | copy-start | bytes 98308
  7.3 54.6 %copy-start.7 = (s32[2]{0:T(128)S(1)}, s32[2]{0:T(128)}, u32[]{:S(2)}) copy-start(s32[2]{0:T(128)} %param.18) | copy-start | bytes 28
  13.5 1.0 copy-start
  15.1 52.0 %all-to-all-start.1 = ((bf16[4,2,512]{2,1,0:T(2,128)(2,1)}), bf16[4,2,512]{2,1,0:T(2,128)(2,1)S(1)}, u32[]{:S(2)}, u32[]{:S(2)}) async-start(bf16[4,2,512]{2,1,0:T(2,128)(2,1)} %all_to_all.41), calls=%async_computation.2 | async-start | bytes 16384 | tf_op jit(solution)/shard_map/all_to_all | solution.py:142
  21.4 66.7 %all-gather.2.cloned.1.call-start = ((), (), s32[]{:S(2)}) async-start(), calls=%async_computation.5 | async-start | bytes 1310720 | tf_op jit(solution)/shard_map/all_gather | solution.py:134
  35.7 26.8 %collective-permute-start.3 = (f32[8]{0:T(128)S(1)}, f32[8]{0:T(128)S(1)}, u32[]{:S(2)}, u32[]{:S(2)}) collective-permute-start(f32[8]{0:T(128)S(1)} %fusion.4), channel_id=1, source_target_pairs={{0,1},{1,0},{2,3},{3,2},{4,5},{5,4},{6,7},{7,6},{8,9},{9,8},{10,11... | collective-permute-start | bytes 104 | tf_op jit(solution)/shard_map/ppermute | solution.py:91
  43.1 9.8 %collective-permute-start = (bf16[64,2048]{1,0:T(8,128)(2,1)}, bf16[64,2048]{1,0:T(8,128)(2,1)S(1)}, u32[]{:S(2)}, u32[]{:S(2)}) collective-permute-start(bf16[64,2048]{1,0:T(8,128)(2,1)} %reduce-scatter.2.cloned.1.call-done), channel_id=1, source_target_pairs={{0,8},{4,12},{8,16},{12,20},{16,24},{20,28},{1,9},{5,13},{9,17},{1... | collective-permute-start | bytes 786440 | tf_op jit(solution)/shard_map/ppermute | solution.py:19
  46.2 12.0 %collective-permute-start.1 = (bf16[64,2048]{1,0:T(8,128)(2,1)}, bf16[64,2048]{1,0:T(8,128)(2,1)S(1)}, u32[]{:S(2)}, u32[]{:S(2)}) collective-permute-start(bf16[64,2048]{1,0:T(8,128)(2,1)} %reduce-scatter.2.cloned.1.call-done), channel_id=1, source_target_pairs={{0,16},{4,20},{8,24},{12,28},{1,17},{5,21},{9,25},{13,29},{2,18},{... | collective-permute-start | bytes 786440 | tf_op jit(solution)/shard_map/ppermute | solution.py:19
  49.6 8.6 %collective-permute-start.2 = (bf16[64,2048]{1,0:T(8,128)(2,1)}, bf16[64,2048]{1,0:T(8,128)(2,1)S(1)}, u32[]{:S(2)}, u32[]{:S(2)}) collective-permute-start(bf16[64,2048]{1,0:T(8,128)(2,1)} %reduce-scatter.2.cloned.1.call-done), channel_id=1, source_target_pairs={{0,24},{4,28},{1,25},{5,29},{2,26},{6,30},{3,27},{7,31}} | collective-permute-start | bytes 786440 | tf_op jit(solution)/shard_map/ppermute | solution.py:19
  62.5 4.5 %collective-permute-start.4 = (f32[8]{0:T(128)S(1)}, f32[8]{0:T(128)S(1)}, u32[]{:S(2)}, u32[]{:S(2)}) collective-permute-start(f32[8]{0:T(128)S(1)} %add.67), channel_id=1, source_target_pairs={{0,2},{1,3},{2,0},{3,1},{4,6},{5,7},{6,4},{7,5},{8,10},{9,11},{10,... | collective-permute-start | bytes 104 | tf_op jit(solution)/shard_map/ppermute | solution.py:91
  67.1 9.3 %all-to-all-start = ((bf16[4,2,2048]{2,1,0:T(2,128)(2,1)}), bf16[4,2,2048]{2,1,0:T(2,128)(2,1)S(1)}, u32[]{:S(2)}, u32[]{:S(2)}) async-start(bf16[4,2,2048]{2,1,0:T(2,128)(2,1)} %all_to_all.38), calls=%async_computation.1 | async-start | bytes 65536 | tf_op jit(solution)/shard_map/all_to_all | solution.py:141
  95.6 8.9 %all-to-all-start.2 = ((bf16[2,4,2048]{2,0,1:T(2,128)(2,1)}), bf16[2,4,2048]{2,0,1:T(2,128)(2,1)S(1)}, u32[]{:S(2)}, u32[]{:S(2)}) async-start(bf16[2,4,2048]{2,0,1:T(2,128)(2,1)} %copy.38), calls=%async_computation.3 | async-start | bytes 65536 | tf_op jit(solution)/shard_map/all_to_all | solution.py:145
Sparse Core Ops, SparseCore 0:
  14.6 28.4 reduce-scatter.1
  59.1 29.0 all-gather.1
